TPU v7x, 32 devices: a whole 2x2x4 slice. The times are simulated.
32 devices in a mesh: loop: 8 (over z, x), rep: 4 (over y, core).
Axes of the slice: x: 2, y: 2, z: 4, core: 2. Of those that a mesh axis runs over, the one named last changes fastest.
Arguments:
- features: float32 [4096, 128], P('loop'), may hold values from -6 to 6
- weight: float32 [128, 256], replicated, may hold values from -0.5 to 0.5
- bias: float32 [256], replicated, may hold values from -3 to 3
- tile_values: float32 [512, 128, 128], P(('loop', 'rep')), may hold values from -0.125 to 0.125
- tile_rows: int32 [512], P(('loop', 'rep')), may hold values from 0 to 31, as said below
- tile_cols: int32 [512], P(('loop', 'rep')), may hold values from 0 to 31, as said below
- tile_count: int32 [32], P(('loop', 'rep')), may hold values from 1 to 16, as said below
- cotangent: float32 [4096, 256], P('loop'), may hold values from -0.6 to 0.6
Outputs:
- output: float32 [4096, 256], P('loop')
- grad_features: float32 [4096, 128], P('loop')
- grad_weight: float32 [128, 256], replicated
- grad_bias: float32 [256], replicated
Inputs may be any that keep to these rules, and one draw needn't show every extreme that they name: `tile_rows`: every slot of a device at loop index l names a row block from l * 4 to (l + 1) * 4 - 1. `tile_cols`: for every loop index m, the live slots of one device name at most 2 different column blocks from m * 4 to (m + 1) * 4 - 1; for every loop index some device names exactly 2 of one such range. `tile_count`: for every loop index some device has all 16 slots live.
All inputs are finite; a program needn't handle non-finite values.
Results may differ from a plain program's by a relative error of at most 0.0001.
Values sent between devices are 32-bit elements; how exact they have to be, the bound alone decides.
No kernel may reach another device: no remote copies, remote signals or barrier semaphores. Data moves between devices by JAX's collectives and lax.ppermute only.
A program may use at most 64 MiB of HBM per device.

v0:
```python
import jax
import jax.numpy as jnp
from jax import lax
from jax.sharding import PartitionSpec as P


def per_device(features, weight, bias, tile_values, tile_rows, tile_cols, tile_count, cotangent):
    highest = lax.Precision.HIGHEST
    tile_side = tile_values.shape[1]
    rows_here = features.shape[0]
    nblocks = rows_here // tile_side
    slots = tile_values.shape[0]
    local_rows = tile_rows - lax.axis_index("loop") * nblocks
    live_slot = (jnp.arange(slots, dtype=jnp.int32) < tile_count[0]).astype(jnp.float32)
    row_pick = (local_rows[:, None] == jnp.arange(nblocks, dtype=jnp.int32)[None, :]).astype(
        jnp.float32
    )
    row_pick = row_pick * live_slot[:, None]
    gathered = lax.all_gather(features, "loop", axis=0, tiled=True)
    width = gathered.shape[1]
    blocks = gathered.reshape(-1, tile_side, width)[tile_cols]
    products = jnp.einsum("kij,kjf->kif", tile_values, blocks, precision=highest)
    aggregated = lax.psum(
        jnp.einsum("kb,kif->bif", row_pick, products, precision=highest), "rep"
    ).reshape(rows_here, -1)
    preactive = jnp.dot(aggregated, weight, precision=highest) + bias
    logistic = jax.nn.sigmoid(preactive)
    output = preactive * logistic
    gradient = cotangent * logistic * (1.0 + preactive * (1.0 - logistic))
    spread = jnp.dot(gradient, weight.T, precision=highest)
    source_blocks = spread.reshape(nblocks, tile_side, spread.shape[1])[
        jnp.clip(local_rows, 0, nblocks - 1)
    ]
    outgoing = jnp.einsum("kji,kjf->kif", tile_values, source_blocks, precision=highest)
    outgoing = outgoing * live_slot[:, None, None]
    span = rows_here * lax.axis_size("loop") // tile_side + 2
    column_pick = (tile_cols[:, None] == jnp.arange(span, dtype=jnp.int32)[None, :]).astype(
        jnp.float32
    )
    placed = jnp.einsum("kb,kif->bif", column_pick, outgoing, precision=highest)
    placed = placed.reshape(span * tile_side, outgoing.shape[2])
    term = lax.psum_scatter(
        lax.slice_in_dim(placed, 0, rows_here * lax.axis_size("loop"), axis=0),
        "loop",
        scatter_dimension=0,
        tiled=True,
    )
    own_rows = lax.psum(term, "rep")
    weight_term = jnp.dot(aggregated.T, gradient, precision=highest)
    bias_term = jnp.sum(gradient, axis=0)
    grad_weight, grad_bias = lax.psum((weight_term, bias_term), "loop")
    return (output, own_rows, grad_weight, grad_bias)


def solution(mesh):
    return jax.shard_map(
        per_device,
        mesh=mesh,
        in_specs=(
            P("loop", None),
            P(),
            P(),
            P(("loop", "rep"), None, None),
            P(("loop", "rep")),
            P(("loop", "rep")),
            P(("loop", "rep")),
            P("loop", None),
        ),
        out_specs=(P("loop", None), P("loop", None), P(), P()),
        check_vma=False,
    )
```

profile of v0, /device:TPU:0, one launch (start us, length us, event | category | flops | bytes accessed | tf_op | source)
XLA Modules:
  0.0 293.9 jit_solution(1856292996977088046)
XLA Ops:
  7.2 0.7 all-gather.2.cloned.1.call-update
  7.9 0.0 all-reduce.4.cloned.1.call-start
  8.6 0.7 compare_select_fusion.1
  9.3 0.7 compare_select_fusion
  10.0 52.0 %all-gather.2.cloned.1.call-done = f32[4096,128]{1,0:T(8,128)} async-done(((f32[512,128]{1,0:T(8,128)}), f32[4096,128]{1,0:T(8,128)}) %all-gather.2.cloned.1.call-update) | async-done | bytes 2097168 | tf_op jit(solution)/shard_map/all_gather | solution.py:19
  62.0 2.2 gather_fusion
  64.2 1.8 fusion.16
  66.1 0.5 copy.14
  66.6 0.6 fusion.2
  67.2 0.7 copy.12
  68.0 0.0 reduce-scatter.2.cloned.1.call-start
  68.0 0.1 fusion.7
  68.1 30.8 %all-reduce.4.cloned.1.call-done = f32[512,128]{1,0:T(8,128)} async-done(((f32[512,128]{1,0:T(8,128)}), f32[512,128]{1,0:T(8,128)}) %all-reduce.4.cloned.1.call-update) | async-done | bytes 262160 | tf_op jit(solution)/shard_map/psum | solution.py:23
  98.9 2.5 fusion.15
  101.4 0.6 fusion.17
  102.0 0.2 copy-done.1
  102.2 0.6 gather_fusion.1
  102.8 1.8 fusion.18
  104.7 0.5 copy.15
  105.2 1.0 fusion
  106.2 2.6 copy.13
  108.8 0.0 all-reduce.8.cloned.1.call-start
  108.9 1.0 copy-done.2
  109.8 0.1 copy-done.3
  109.9 1.3 fusion.19
  111.2 0.0 all-reduce.6.cloned.1.call-start
  111.3 66.0 %reduce-scatter.2.cloned.1.call-done = f32[512,128]{1,0:T(8,128)} async-done(((f32[4096,128]{1,0:T(8,128)}), f32[512,128]{1,0:T(8,128)}) %reduce-scatter.2.cloned.1.call-update) | async-done | bytes 262160 | tf_op jit(solution)/shard_map/reduce_scatter | solution.py:42
  177.3 19.7 %psum.31 = f32[256]{0:T(256)} all-reduce(f32[256]{0:T(256)S(1)} %get-tuple-element.4), channel_id=1, replica_groups=mesh['loop'=8,'rep'=4] {'loop'}, use_global_device_ids=true, to_apply=%region_5.6 | all-reduce | flops 256 | bytes 2048 | tf_op jit(solution)/shard_map/psum | solution.py:51
  197.0 53.6 %all-reduce.8.cloned.1.call-done = f32[128,256]{1,0:T(8,128)} async-done(((f32[128,256]{1,0:T(8,128)}), f32[128,256]{1,0:T(8,128)}) %all-reduce.8.cloned.1.call-update) | async-done | bytes 131088 | tf_op jit(solution)/shard_map/psum | solution.py:51
  250.6 33.6 %all-reduce.6.cloned.1.call-done = f32[512,128]{1,0:T(8,128)} async-done(((f32[512,128]{1,0:T(8,128)}), f32[512,128]{1,0:T(8,128)}) %all-reduce.6.cloned.1.call-update) | async-done | bytes 262160 | tf_op jit(solution)/shard_map/psum | solution.py:48
  284.2 1.7 copy.20
  285.8 1.6 copy.21
  (21 shorter events, 0.2 us)
Async XLA Ops:
  7.2 57.0 %copy-start = (f32[16,128,128]{2,1,0:T(8,128)S(1)}, f32[16,128,128]{2,1,0:T(8,128)}, u32[]{:S(2)}) copy-start(f32[16,128,128]{2,1,0:T(8,128)} %param.11) | copy-start | bytes 3145732
  7.2 54.8 %all-gather.2.cloned.1.call-start = ((), (), s32[]{:S(2)}) async-start(), calls=%async_computation.1 | async-start | bytes 2359296 | tf_op jit(solution)/shard_map/all_gather | solution.py:19
  7.9 91.0 %all-reduce.4.cloned.1.call-start = ((), (), s32[]{:S(2)}) async-start(), calls=%async_computation.2 | async-start | bytes 524288 | tf_op jit(solution)/shard_map/psum | solution.py:23
  66.0 2.0 copy-start.5
  66.0 32.9 %copy-start.4 = (f32[128,256]{1,0:T(8,128)S(1)}, f32[128,256]{1,0:T(8,128)}, u32[]{:S(2)}) copy-start(f32[128,256]{1,0:T(8,128)} %param.9) | copy-start | bytes 393220
  66.0 32.9 %copy-start.7 = (f32[256]{0:T(256)S(1)}, f32[256]{0:T(256)}, u32[]{:S(2)}) copy-start(f32[256]{0:T(256)} %param.10) | copy-start | bytes 3076
  66.6 32.4 %copy-start.6 = (f32[512,256]{1,0:T(8,128)S(1)}, f32[512,256]{1,0:T(8,128)}, u32[]{:S(2)}) copy-start(f32[512,256]{1,0:T(8,128)} %param.15) | copy-start | bytes 1572868
  68.0 109.3 %reduce-scatter.2.cloned.1.call-start = ((), (), s32[]{:S(2)}) async-start(), calls=%async_computation.3 | async-start | bytes 2359296 | tf_op jit(solution)/shard_map/reduce_scatter | solution.py:42
  101.4 0.8 copy-start.1
  108.8 1.0 copy-start.2
  108.8 1.1 copy-start.3
  108.8 141.7 %all-reduce.8.cloned.1.call-start = ((), (), s32[]{:S(2)}) async-start(), calls=%async_computation.5 | async-start | bytes 262144 | tf_op jit(solution)/shard_map/psum | solution.py:51
  111.2 173.0 %all-reduce.6.cloned.1.call-start = ((), (), s32[]{:S(2)}) async-start(), calls=%async_computation.4 | async-start | bytes 524288 | tf_op jit(solution)/shard_map/psum | solution.py:48
Sparse Core Ops, SparseCore 0:
  10.1 51.7 all-gather.1
  68.1 30.8 all-reduce.3
  108.9 68.2 reduce-scatter.1
  181.0 69.4 all-reduce.7
  252.7 31.3 all-reduce.5
where the time goes:
time: 294 us
  waiting for transfers between devices  237 us (81%)
  blocking collectives  19.7 us (7%)
  between operations  14.6 us (5%)
  local copies, waits for them, and re-layouts  11.6 us (4%)
  matrix products  9.66 us (3%)
    reduce_scatter x1, waiting for transfers between devices, per_device(): lax.psum_scatter(lax.slice_in_dim(placed, 0, rows_here * lax.axis_size('l...  66 us
    psum x1, waiting for transfers between devices, per_device(): grad_weight, grad_bias = lax.psum((weight_term, bias_term), 'loop')  53.6 us
    all_gather x1, waiting for transfers between devices, per_device(): gathered = lax.all_gather(features, 'loop', axis=0, tiled=True)  52 us
    psum x1, waiting for transfers between devices, per_device(): own_rows = lax.psum(term, 'rep')  33.6 us
    psum x1, waiting for transfers between devices, per_device(): lax.psum(jnp.einsum('kb,kif->bif', row_pick, products, precision=highest)...  30.8 us
    psum x1, blocking collectives, per_device(): grad_weight, grad_bias = lax.psum((weight_term, bias_term), 'loop')  19.7 us
  transfers between devices with their start and end apart: 5, of which 5 were waited for; matrix products, arithmetic and copies ran while one was open for 1% of the time, Pallas kernels for 0%

commit v1 on v0

--- a/solution.py
+++ b/solution.py
@@ -45,7 +45,7 @@
         scatter_dimension=0,
         tiled=True,
     )
-    own_rows = lax.psum(term, "rep")
+    own_rows = lax.all_gather(term, axis_name="rep").sum(axis=0)
     weight_term = jnp.dot(aggregated.T, gradient, precision=highest)
     bias_term = jnp.sum(gradient, axis=0)
     grad_weight, grad_bias = lax.psum((weight_term, bias_term), "loop")

time: 294 us -> 277 us (0.942)
  waiting for transfers between devices: 237 us -> 220 us
    psum x1 -> x0, waiting for transfers between devices: 33.6 us -> none  [per_device(): own_rows = lax.psum(term, 'rep')]
    psum x1, waiting for transfers between devices: 53.6 us -> 68.4 us  [per_device(): grad_weight, grad_bias = lax.psum((weight_term, bias_term), 'loop')]
  transfers between devices with their start and end apart: 5 -> 5, of which waited for: 5 -> 4; matrix products, arithmetic and copies ran while one was open for 1% -> 2% of each run, Pallas kernels for 0% -> 0%
where the time goes in v1:
time: 277 us
  waiting for transfers between devices  220 us (79%)
  blocking collectives  19.6 us (7%)
  between operations  14.6 us (5%)
  matrix products  9.67 us (3%)
  local copies, waits for them, and re-layouts  8.94 us (3%)
  other arithmetic  3.42 us (1%)
    reduce_scatter x1, waiting for transfers between devices, per_device(): lax.psum_scatter(lax.slice_in_dim(placed, 0, rows_here * lax.axis_size('l...  68.4 us
    psum x1, waiting for transfers between devices, per_device(): grad_weight, grad_bias = lax.psum((weight_term, bias_term), 'loop')  68.4 us
    all_gather x1, waiting for transfers between devices, per_device(): gathered = lax.all_gather(features, 'loop', axis=0, tiled=True)  52 us
    psum x1, waiting for transfers between devices, per_device(): lax.psum(jnp.einsum('kb,kif->bif', row_pick, products, precision=highest)...  30.8 us
    psum x1, blocking collectives, per_device(): grad_weight, grad_bias = lax.psum((weight_term, bias_term), 'loop')  19.6 us
  transfers between devices with their start and end apart: 5, of which 4 were waited for; matrix products, arithmetic and copies ran while one was open for 2% of the time, Pallas kernels for 0%

profile of v1, /device:TPU:0, one launch (start us, length us, event | category | flops | bytes accessed | tf_op | source)
XLA Modules:
  0.0 276.8 jit_solution(13177024379857865149)
XLA Ops:
  7.2 0.0 all-gather.4.cloned.1.call-start
  7.2 0.7 all-gather.4.cloned.1.call-update
  7.9 0.0 all-reduce.3.cloned.1.call-start
  8.6 0.7 compare_select_fusion.1
  9.3 0.7 compare_select_fusion
  10.0 52.0 %all-gather.4.cloned.1.call-done = f32[4096,128]{1,0:T(8,128)} async-done(((f32[512,128]{1,0:T(8,128)}), f32[4096,128]{1,0:T(8,128)}) %all-gather.4.cloned.1.call-update) | async-done | bytes 2097168 | tf_op jit(solution)/shard_map/all_gather | solution.py:19
  62.0 2.2 gather_fusion
  64.2 1.8 fusion.16
  66.1 0.5 copy.14
  66.6 0.6 fusion.2
  67.2 0.7 copy.12
  67.9 0.0 all-reduce.3.cloned.1.call-update
  68.0 0.0 reduce-scatter.2.cloned.1.call-start
  68.0 0.1 fusion.7
  68.1 30.8 %all-reduce.3.cloned.1.call-done = f32[512,128]{1,0:T(8,128)} async-done(((f32[512,128]{1,0:T(8,128)}), f32[512,128]{1,0:T(8,128)}) %all-reduce.3.cloned.1.call-update) | async-done | bytes 262160 | tf_op jit(solution)/shard_map/psum | solution.py:23
  98.9 2.5 fusion.15
  101.4 0.6 fusion.17
  102.0 0.2 copy-done.1
  102.2 0.6 gather_fusion.1
  102.8 1.8 fusion.18
  104.7 0.5 copy.15
  105.2 1.0 fusion
  106.2 2.6 copy.13
  108.8 0.0 reduce-scatter.2.cloned.1.call-update
  108.8 0.0 all-gather.6.cloned.1.call-start
  108.9 68.4 %reduce-scatter.2.cloned.1.call-done = f32[512,128]{1,0:T(8,128)} async-done(((f32[4096,128]{1,0:T(8,128)}), f32[512,128]{1,0:T(8,128)}) %reduce-scatter.2.cloned.1.call-update) | async-done | bytes 262160 | tf_op jit(solution)/shard_map/reduce_scatter | solution.py:42
  177.3 0.0 all-reduce.5.cloned.1.call-start
  177.3 1.3 fusion.19
  178.6 19.6 %psum.23 = f32[256]{0:T(256)} all-reduce(f32[256]{0:T(256)S(1)} %get-tuple-element.4), channel_id=1, replica_groups=mesh['loop'=8,'rep'=4] {'loop'}, use_global_device_ids=true, to_apply=%region_5.6 | all-reduce | flops 256 | bytes 2048 | tf_op jit(solution)/shard_map/psum | solution.py:51
  198.3 2.0 reduce_sum.18
  200.3 68.4 %all-reduce.5.cloned.1.call-done = f32[128,256]{1,0:T(8,128)} async-done(((f32[128,256]{1,0:T(8,128)}), f32[128,256]{1,0:T(8,128)}) %all-reduce.5.cloned.1.call-update) | async-done | bytes 131088 | tf_op jit(solution)/shard_map/psum | solution.py:51
  268.7 1.6 copy.19
  (21 shorter events, 0.1 us)
Async XLA Ops:
  7.2 57.0 %copy-start = (f32[16,128,128]{2,1,0:T(8,128)S(1)}, f32[16,128,128]{2,1,0:T(8,128)}, u32[]{:S(2)}) copy-start(f32[16,128,128]{2,1,0:T(8,128)} %param.11) | copy-start | bytes 3145732
  7.2 54.8 %all-gather.4.cloned.1.call-start = ((), (), s32[]{:S(2)}) async-start(), calls=%async_computation.1 | async-start | bytes 2359296 | tf_op jit(solution)/shard_map/all_gather | solution.py:19
  7.9 91.0 %all-reduce.3.cloned.1.call-start = ((), (), s32[]{:S(2)}) async-start(), calls=%async_computation.2 | async-start | bytes 524288 | tf_op jit(solution)/shard_map/psum | solution.py:23
  66.0 2.0 copy-start.5
  66.0 32.9 %copy-start.4 = (f32[128,256]{1,0:T(8,128)S(1)}, f32[128,256]{1,0:T(8,128)}, u32[]{:S(2)}) copy-start(f32[128,256]{1,0:T(8,128)} %param.9) | copy-start | bytes 393220
  66.0 32.9 %copy-start.7 = (f32[256]{0:T(256)S(1)}, f32[256]{0:T(256)}, u32[]{:S(2)}) copy-start(f32[256]{0:T(256)} %param.10) | copy-start | bytes 3076
  66.6 32.4 %copy-start.6 = (f32[512,256]{1,0:T(8,128)S(1)}, f32[512,256]{1,0:T(8,128)}, u32[]{:S(2)}) copy-start(f32[512,256]{1,0:T(8,128)} %param.15) | copy-start | bytes 1572868
  68.0 109.3 %reduce-scatter.2.cloned.1.call-start = ((), (), s32[]{:S(2)}) async-start(), calls=%async_computation.3 | async-start | bytes 2359296 | tf_op jit(solution)/shard_map/reduce_scatter | solution.py:42
  101.4 0.8 copy-start.1
  108.8 68.5 %copy-start.2 = (f32[512,256]{1,0:T(8,128)S(1)}, f32[512,256]{1,0:T(8,128)}, u32[]{:S(2)}) copy-start(f32[512,256]{1,0:T(8,128)} %copy-done.1) | copy-start | bytes 1572868
  108.8 68.5 %copy-start.3 = (f32[512,128]{1,0:T(8,128)S(1)}, f32[512,128]{1,0:T(8,128)}, u32[]{:S(2)}) copy-start(f32[512,128]{1,0:T(8,128)} %all-reduce.3.cloned.1.call-done) | copy-start | bytes 786436
  108.8 89.5 %all-gather.6.cloned.1.call-start = ((), (), s32[]{:S(2)}) async-start(), calls=%async_computation.5 | async-start | bytes 1310720 | tf_op jit(solution)/shard_map/all_gather | solution.py:48
  177.3 91.4 %all-reduce.5.cloned.1.call-start = ((), (), s32[]{:S(2)}) async-start(), calls=%async_computation.4 | async-start | bytes 262144 | tf_op jit(solution)/shard_map/psum | solution.py:51
Sparse Core Ops, SparseCore 0:
  10.1 51.7 all-gather.3
  68.1 30.8 all-reduce.2
  108.9 68.2 reduce-scatter.1
  178.7 15.6 all-gather.5
  198.2 70.4 all-reduce.4
